TPU v7x, 128 devices: a whole 4x4x4 slice. The times are simulated.
128 devices in a mesh: row: 16 (over z, x_hi, core), col: 8 (over y, x_lo).
Axes of the slice: x: 4 (x_hi: 2, x_lo: 2; x = x_hi * 2 + x_lo), y: 4, z: 4, core: 2. Of those that a mesh axis runs over, the one named last changes fastest.
Arguments:
- momentum_shards: bfloat16 [6656, 18432], P(('row', 'col')), may hold values from -0.078125 to 0.078125
- shard_starts: int32 [128], replicated, may hold values from 0 to 3568, as said below
Outputs:
- update_shards: bfloat16 [6656, 18432], P(('row', 'col'))
Inputs may be any that keep to these rules, and one draw needn't show every extreme that they name: `shard_starts`: starts never fall and the first is 0; shard d starts within 12 rows of d * 28, and the last one exactly 12 rows after it. Every shard has at most 52 rows and some shard has exactly 52; the 8 shards of one index of row hold at most 248 rows together, and on some index exactly 248.
All inputs are finite; a program needn't handle non-finite values.
Results may differ from a plain program's by a relative error of at most 0.02.
Values may be sent and summed in bfloat16 or wider, within the bound.
A program may use at most 128 MiB of HBM per device.

v0:
```python
import math
import jax
import jax.numpy as jnp
from jax import lax
from jax.sharding import PartitionSpec as P

M = 3584
N = 18432
coef_one = 3.4445
coef_two = -4.775
coef_three = 2.0315


def in_blocks(value, dim, size):
    shape = value.shape
    tiles = value.reshape(*shape[:dim], size, shape[dim] // size, *shape[dim + 1 :])
    return jnp.moveaxis(tiles, dim, 0)


def summed_on_arrival(value, axis, dim):
    size = lax.axis_size(axis)
    tiles = lax.all_to_all(in_blocks(value, dim, size), axis, 0, 0, tiled=True)
    return jnp.sum(tiles.astype(jnp.float32), axis=0)


def laid_out(tiles, dim):
    shape = list(tiles.shape[1:])
    shape[dim] *= tiles.shape[0]
    return jnp.moveaxis(tiles, 0, dim).reshape(shape)


def sent_to_all(value, axis):
    copies = jnp.broadcast_to(value, (lax.axis_size(axis), *value.shape))
    return lax.all_to_all(copies, axis, split_axis=0, concat_axis=0, tiled=True)


def gather_directly(value, axis, dim):
    return laid_out(sent_to_all(value, axis), dim)


def packing(shard_starts, row_block, col_count, shard_rows, window):
    shard_ends = jnp.concatenate([shard_starts[1:], jnp.full((1,), M, jnp.int32)])
    first_starts = lax.dynamic_slice_in_dim(shard_starts, row_block * col_count, col_count)
    last_ends = lax.dynamic_slice_in_dim(shard_ends, row_block * col_count, col_count)
    slot_index = jnp.arange(col_count * shard_rows, dtype=jnp.int32)
    member = slot_index // shard_rows
    offset = slot_index % shard_rows
    pick = member[:, None] == jnp.arange(col_count, dtype=jnp.int32)[None, :]
    shard_begin = jnp.sum(jnp.where(pick, first_starts[None, :], 0), axis=1)
    length = jnp.sum(jnp.where(pick, (last_ends - first_starts)[None, :], 0), axis=1)
    target = shard_begin - first_starts[0] + offset
    is_valid = offset < length
    window_rows = jnp.arange(window, dtype=jnp.int32)
    return ((window_rows[:, None] == target[None, :]) & is_valid[None, :]).astype(jnp.bfloat16)


def body(momentum_shards, shard_starts):
    col_count = lax.axis_size("col")
    row_count = lax.axis_size("row")
    shard_rows = momentum_shards.shape[0]
    mean_rows = M // (row_count * col_count)
    jitter = 4 * (mean_rows // 8)
    window = col_count * mean_rows + 2 * jitter
    packer = packing(shard_starts, lax.axis_index("row"), col_count, shard_rows, window)
    columns = lax.all_to_all(momentum_shards, "col", split_axis=1, concat_axis=0, tiled=True)
    local_tile = jnp.dot(packer, columns, preferred_element_type=jnp.float32).astype(jnp.bfloat16)
    col_panel = lax.all_gather(local_tile, "row", axis=0, tiled=True)
    own_block = summed_on_arrival(
        lax.dot_general(
            col_panel, local_tile, (((1,), (1,)), ((), ())), preferred_element_type=jnp.float32
        ).astype(jnp.bfloat16),
        "col",
        0,
    ).astype(jnp.bfloat16)
    across = lax.all_gather(own_block, "row", axis=1, tiled=True)
    square_own = summed_on_arrival(
        lax.dot_general(
            across, own_block, (((0,), (0,)), ((), ())), preferred_element_type=jnp.float32
        ).astype(jnp.bfloat16),
        "col",
        0,
    )
    poly_own = (coef_two * own_block.astype(jnp.float32) + coef_three * square_own).astype(
        jnp.bfloat16
    )
    poly_block = gather_directly(poly_own, "col", 0)
    mixed_part = lax.dot_general(
        poly_block, col_panel, (((0,), (0,)), ((), ())), preferred_element_type=jnp.float32
    )
    update = (math.sqrt(N) * (coef_one * local_tile.astype(jnp.float32) + mixed_part)).astype(
        jnp.bfloat16
    )
    back_rows = lax.dot_general(
        packer, update, (((0,), (0,)), ((), ())), preferred_element_type=jnp.float32
    ).astype(jnp.bfloat16)
    return lax.all_to_all(back_rows, "col", split_axis=0, concat_axis=1, tiled=True)


def solution(mesh):
    in_specs = (P(("row", "col"), None), P())
    out_specs = P(("row", "col"), None)
    return jax.shard_map(body, mesh=mesh, in_specs=in_specs, out_specs=out_specs, check_vma=False)
```

profile of v0, /device:TPU:0, one launch (start us, length us, event | category | flops | bytes accessed | tf_op | source)
XLA Modules:
  0.0 387.3 jit_solution(3728973360433823546)
XLA Ops:
  6.5 1.9 copy.23
  8.6 1.6 copy.14
  10.2 5.6 %all-to-all-start = ((bf16[52,8,2304]{2,0,1:T(8,128)(2,1)}), bf16[52,8,2304]{2,0,1:T(8,128)(2,1)S(1)}, u32[]{:S(2)}, u32[]{:S(2)}) async-start(bf16[52,8,2304]{2,0,1:T(8,128)(2,1)} %copy.14), calls=%async_computation | async-start | bytes 4128768 | tf_op jit(solution)/shard_map/all_to_all | solution.py:65
  16.3 26.2 %all-to-all-done = bf16[52,8,2304]{2,0,1:T(8,128)(2,1)S(1)} async-done(((bf16[52,8,2304]{2,0,1:T(8,128)(2,1)}), bf16[52,8,2304]{2,0,1:T(8,128)(2,1)S(1)}, u32[]{:S(2)}, u32[]{:S(2)}) %all-to-all-start) | async-done | bytes 1916960 | tf_op jit(solution)/shard_map/all_to_all | solution.py:65
  42.5 1.4 all_to_all.40
  43.9 3.3 convolution_convert_fusion.3
  47.3 116.2 %all-gather.3.cloned.1.call-done = bf16[3968,2304]{1,0:T(8,128)(2,1)} async-done(((bf16[248,2304]{1,0:T(8,128)(2,1)}), bf16[3968,2304]{1,0:T(8,128)(2,1)}) %all-gather.3.cloned.1.call-update) | async-done | bytes 18284560 | tf_op jit(solution)/shard_map/all_gather | solution.py:67
  163.5 12.8 %convolution_convert_fusion.1 = bf16[3968,248]{0,1:T(8,128)(2,1)} fusion(bf16[3968,2304]{1,0:T(8,128)(2,1)} %all-gather.3.cloned.1.call-done, bf16[248,2304]{1,0:T(8,128)(2,1)} %convolution_convert_fusion.3), kind=kOutput, calls=%fused_computation.1 | convolution fusion | flops 4535550976 | bytes 21395456 | tf_op jit(solution)/shard_map/dot_general | solution.py:69
  176.3 5.6 %reshape.48 = bf16[8,496,248]{1,0,2:T(8,128)(2,1)S(1)} reshape(bf16[3968,248]{0,1:T(8,128)(2,1)} %convolution_convert_fusion.1) | data formatting | bytes 3936256 | tf_op jit(solution)/shard_map/reshape | solution.py:16
  181.9 0.7 copy.15
  182.6 30.8 %all_to_all.53 = bf16[8,496,248]{1,2,0:T(8,128)(2,1)S(1)} all-to-all(bf16[8,496,248]{1,2,0:T(8,128)(2,1)S(1)} %copy.15), channel_id=1, replica_groups=mesh['row'=16,'col'=8] {'col'}, dimensions={0} | all-to-all | bytes 3936256 | tf_op jit(solution)/shard_map/all_to_all | solution.py:22
  213.3 1.1 reduce_sum.41
  214.4 51.3 %all-gather.5.cloned.1.call-done = bf16[496,3968]{0,1:T(8,128)(2,1)} async-done(((bf16[496,248]{0,1:T(8,128)(2,1)}), bf16[496,3968]{0,1:T(8,128)(2,1)}) %all-gather.5.cloned.1.call-update) | async-done | bytes 3936272 | tf_op jit(solution)/shard_map/all_gather | solution.py:75
  265.7 4.7 %convolution_convert_fusion = bf16[3968,248]{0,1:T(8,128)(2,1)} fusion(bf16[496,3968]{0,1:T(8,128)(2,1)} %all-gather.5.cloned.1.call-done, bf16[496,248]{0,1:T(8,128)(2,1)} %reduce_sum.41), kind=kOutput, calls=%fused_computation | convolution fusion | flops 977175552 | bytes 6150400 | tf_op jit(solution)/shard_map/dot_general | solution.py:77
  270.5 5.6 %reshape.49 = bf16[8,496,248]{1,0,2:T(8,128)(2,1)S(1)} reshape(bf16[3968,248]{0,1:T(8,128)(2,1)} %convolution_convert_fusion) | data formatting | bytes 3936256 | tf_op jit(solution)/shard_map/reshape | solution.py:16
  276.0 0.7 copy.17
  276.7 30.8 %all_to_all.54 = bf16[8,496,248]{1,2,0:T(8,128)(2,1)S(1)} all-to-all(bf16[8,496,248]{1,2,0:T(8,128)(2,1)S(1)} %copy.17), channel_id=1, replica_groups=mesh['row'=16,'col'=8] {'col'}, dimensions={0} | all-to-all | bytes 3936256 | tf_op jit(solution)/shard_map/all_to_all | solution.py:22
  307.5 0.3 convert_reduce_fusion
  307.8 0.6 copy-done
  308.8 28.6 %all_to_all.55 = bf16[8,496,248]{2,1,0:T(8,128)(2,1)S(1)} all-to-all(bf16[8,496,248]{2,1,0:T(8,128)(2,1)S(1)} %broadcast_in_dim.31), channel_id=1, replica_groups=mesh['row'=16,'col'=8] {'col'}, dimensions={0} | all-to-all | bytes 3936256 | tf_op jit(solution)/shard_map/all_to_all | solution.py:34
  337.4 11.1 %convolution_convert_fusion.2 = bf16[416,2304]{1,0:T(8,128)(2,1)} fusion(s32[416]{0:T(512)S(1)} %subtract_add_fusion, pred[416]{0:T(512)(128)(4,1)S(1)} %fusion.16, bf16[3968,248]{1,0:T(8,128)(2,1)S(1)} %bitcast.27, bf16[3968,2304]{1,0:T(8,128)(2,1)} %all-gather.3.cloned.1.call-done, bf16[248,2304]{1,0:T(8,128)(2,1)S(1)} %copy-done.1), kind=kOutput, calls=%fused_computation.2 | convolution fusion | flops 5013986816 | bytes 23314464 | tf_op jit(solution)/shard_map/dot_general | solution.py:93
  348.5 1.7 all_to_all.44
  350.2 28.1 %all_to_all.56 = bf16[8,52,2304]{2,1,0:T(8,128)(2,1)S(1)} all-to-all(bf16[8,52,2304]{2,1,0:T(8,128)(2,1)S(1)} %all_to_all.44), channel_id=1, replica_groups=mesh['row'=16,'col'=8] {'col'}, dimensions={0} | all-to-all | bytes 3833856 | tf_op jit(solution)/shard_map/all_to_all | solution.py:96
  378.8 1.7 copy.24
  (22 shorter events, 1.4 us)
Async XLA Ops:
  10.2 5.7 %copy-start.2 = (s32[128]{0:T(128)S(1)}, s32[128]{0:T(128)}, u32[]{:S(2)}) copy-start(s32[128]{0:T(128)} %param.3) | copy-start | bytes 1540
  10.2 32.3 %all-to-all-start = ((bf16[52,8,2304]{2,0,1:T(8,128)(2,1)}), bf16[52,8,2304]{2,0,1:T(8,128)(2,1)S(1)}, u32[]{:S(2)}, u32[]{:S(2)}) async-start(bf16[52,8,2304]{2,0,1:T(8,128)(2,1)} %copy.14), calls=%async_computation | async-start | bytes 4128768 | tf_op jit(solution)/shard_map/all_to_all | solution.py:65
  15.9 147.7 %all-gather.3.cloned.1.call-start = ((), (), s32[]{:S(2)}) async-start(), calls=%async_computation.5 | async-start | bytes 19427328 | tf_op jit(solution)/shard_map/all_gather | solution.py:67
  47.3 218.4 %all-gather.5.cloned.1.call-start = ((), (), s32[]{:S(2)}) async-start(), calls=%async_computation.6 | async-start | bytes 4317184 | tf_op jit(solution)/shard_map/all_gather | solution.py:75
  307.5 0.9 copy-start
  308.8 28.6 %copy-start.1 = (bf16[248,2304]{1,0:T(8,128)(2,1)S(1)}, bf16[248,2304]{1,0:T(8,128)(2,1)}, u32[]{:S(2)}) copy-start(bf16[248,2304]{1,0:T(8,128)(2,1)} %convolution_convert_fusion.3) | copy-start | bytes 3428356
Sparse Core Ops, SparseCore 0:
  47.4 116.0 all-gather.2
  214.6 51.1 all-gather.4
where the time goes:
time: 388 us; the launch traced here: 387 us
  waiting for transfers between devices  194 us (50%)
  blocking collectives  118 us (30%)
  matrix products  32 us (8%)
  local copies, waits for them, and re-layouts  22.3 us (6%)
  between operations  13.5 us (3%)
  starting transfers between devices  5.72 us (1%)
    all_gather x1, waiting for transfers between devices, body(): col_panel = lax.all_gather(local_tile, 'row', axis=0, tiled=True)  116 us
    all_to_all x2, blocking collectives, summed_on_arrival(): tiles = lax.all_to_all(in_blocks(value, dim, size), axis, 0, 0, tiled=True)  61.5 us
    all_gather x1, waiting for transfers between devices, body(): across = lax.all_gather(own_block, 'row', axis=1, tiled=True)  51.3 us
    all_to_all x1, blocking collectives, sent_to_all(): return lax.all_to_all(copies, axis, split_axis=0, concat_axis=0, tiled=True)  28.6 us
    all_to_all x1, blocking collectives, body(): lax.all_to_all(back_rows, 'col', split_axis=0, concat_axis=1, tiled=True)  28.1 us
    all_to_all x1, waiting for transfers between devices, body(): lax.all_to_all(momentum_shards, 'col', split_axis=1, concat_axis=0, tiled...  26.2 us
    dot_general x1, matrix products, body(): lax.dot_general(col_panel, local_tile, (((1,), (1,)), ((), ())), preferre...  12.8 us
    reshape x4, local copies, waits for them, and re-layouts, in_blocks(): value.reshape(*shape[:dim], size, shape[dim] // size, *shape[dim + 1:])  12.5 us
  transfers between devices with their start and end apart: 3, of which 3 were waited for; matrix products, arithmetic and copies ran while one was open for 0% of the time, Pallas kernels for 0%

commit v1 on v0

--- a/solution.py
+++ b/solution.py
@@ -72,7 +72,9 @@
         "col",
         0,
     ).astype(jnp.bfloat16)
-    across = lax.all_gather(own_block, "row", axis=1, tiled=True)
+    across = jnp.concatenate(
+        lax.all_to_all(jnp.stack([own_block] * lax.axis_size("row")), "row", 0, 0), axis=1
+    )
     square_own = summed_on_arrival(
         lax.dot_general(
             across, own_block, (((0,), (0,)), ((), ())), preferred_element_type=jnp.float32

time: 388 us -> 384 us (0.990)
  waiting for transfers between devices: 194 us -> 142 us
  blocking collectives: 118 us -> 169 us
    all_to_all x0 -> x1, blocking collectives: none -> 54.2 us  [body(): lax.all_to_all(jnp.stack([own_block] * lax.axis_size('row')), 'row', 0, 0)]
    all_gather x1 -> x0, waiting for transfers between devices: 51.3 us -> none  [body(): across = lax.all_gather(own_block, 'row', axis=1, tiled=True)]
  transfers between devices with their start and end apart: 3 -> 2, of which waited for: 3 -> 2; matrix products, arithmetic and copies ran while one was open for 0% -> 0% of each run, Pallas kernels for 0% -> 0%
where the time goes in v1:
time: 384 us; the launch traced here: 383 us
  blocking collectives  169 us (44%)
  waiting for transfers between devices  142 us (37%)
  matrix products  29.6 us (8%)
  local copies, waits for them, and re-layouts  22 us (6%)
  between operations  13.5 us (4%)
  starting transfers between devices  5.68 us (1%)
    all_gather x1, waiting for transfers between devices, body(): col_panel = lax.all_gather(local_tile, 'row', axis=0, tiled=True)  116 us
    all_to_all x2, blocking collectives, summed_on_arrival(): tiles = lax.all_to_all(in_blocks(value, dim, size), axis, 0, 0, tiled=True)  59.2 us
    all_to_all x1, blocking collectives, body(): lax.all_to_all(jnp.stack([own_block] * lax.axis_size('row')), 'row', 0, 0)  54.2 us
    all_to_all x1, blocking collectives, sent_to_all(): return lax.all_to_all(copies, axis, split_axis=0, concat_axis=0, tiled=True)  27.9 us
    all_to_all x1, blocking collectives, body(): lax.all_to_all(back_rows, 'col', split_axis=0, concat_axis=1, tiled=True)  27.4 us
    all_to_all x1, waiting for transfers between devices, body(): lax.all_to_all(momentum_shards, 'col', split_axis=1, concat_axis=0, tiled...  26.2 us
    dot_general x1, matrix products, body(): lax.dot_general(col_panel, local_tile, (((1,), (1,)), ((), ())), preferre...  12.8 us
    reshape x4, local copies, waits for them, and re-layouts, in_blocks(): value.reshape(*shape[:dim], size, shape[dim] // size, *shape[dim + 1:])  12.5 us
  transfers between devices with their start and end apart: 2, of which 2 were waited for; matrix products, arithmetic and copies ran while one was open for 0% of the time, Pallas kernels for 0%

profile of v1, /device:TPU:0, one launch (start us, length us, event | category | flops | bytes accessed | tf_op | source)
XLA Modules:
  0.0 383.1 jit_solution(17242412043610087692)
XLA Ops:
  6.5 1.9 copy.19
  8.6 1.6 copy.14
  10.2 5.6 %all-to-all-start = ((bf16[52,8,2304]{2,0,1:T(8,128)(2,1)}), bf16[52,8,2304]{2,0,1:T(8,128)(2,1)S(1)}, u32[]{:S(2)}, u32[]{:S(2)}) async-start(bf16[52,8,2304]{2,0,1:T(8,128)(2,1)} %copy.14), calls=%async_computation | async-start | bytes 4128768 | tf_op jit(solution)/shard_map/all_to_all | solution.py:65
  16.3 26.2 %all-to-all-done = bf16[52,8,2304]{2,0,1:T(8,128)(2,1)S(1)} async-done(((bf16[52,8,2304]{2,0,1:T(8,128)(2,1)}), bf16[52,8,2304]{2,0,1:T(8,128)(2,1)S(1)}, u32[]{:S(2)}, u32[]{:S(2)}) %all-to-all-start) | async-done | bytes 1916960 | tf_op jit(solution)/shard_map/all_to_all | solution.py:65
  42.5 1.4 all_to_all.43
  43.9 3.3 convolution_convert_fusion.3
  47.3 116.2 %all-gather.2.cloned.1.call-done = bf16[3968,2304]{1,0:T(8,128)(2,1)} async-done(((bf16[248,2304]{1,0:T(8,128)(2,1)}), bf16[3968,2304]{1,0:T(8,128)(2,1)}) %all-gather.2.cloned.1.call-update) | async-done | bytes 18284560 | tf_op jit(solution)/shard_map/all_gather | solution.py:67
  163.5 12.8 %convolution_convert_fusion.1 = bf16[3968,248]{0,1:T(8,128)(2,1)} fusion(bf16[3968,2304]{1,0:T(8,128)(2,1)} %all-gather.2.cloned.1.call-done, bf16[248,2304]{1,0:T(8,128)(2,1)} %convolution_convert_fusion.3), kind=kOutput, calls=%fused_computation.1 | convolution fusion | flops 4535550976 | bytes 21395456 | tf_op jit(solution)/shard_map/dot_general | solution.py:69
  176.3 5.6 %reshape.56 = bf16[8,496,248]{1,0,2:T(8,128)(2,1)S(1)} reshape(bf16[3968,248]{0,1:T(8,128)(2,1)} %convolution_convert_fusion.1) | data formatting | bytes 3936256 | tf_op jit(solution)/shard_map/reshape | solution.py:16
  181.9 0.7 copy.15
  182.5 30.8 %all_to_all.58 = bf16[8,496,248]{1,2,0:T(8,128)(2,1)S(1)} all-to-all(bf16[8,496,248]{1,2,0:T(8,128)(2,1)S(1)} %copy.15), channel_id=1, replica_groups=mesh['row'=16,'col'=8] {'col'}, dimensions={0} | all-to-all | bytes 3936256 | tf_op jit(solution)/shard_map/all_to_all | solution.py:22
  213.3 0.4 reduce_sum.41
  214.0 54.2 %all_to_all.59 = bf16[16,496,248]{1,2,0:T(8,128)(2,1)S(1)} all-to-all(bf16[16,496,248]{1,2,0:T(8,128)(2,1)S(1)} %stack.2), channel_id=1, replica_groups=mesh['row'=16,'col'=8] {'row'}, dimensions={0} | all-to-all | bytes 7872512 | tf_op jit(solution)/shard_map/all_to_all | solution.py:76
  268.2 2.6 convolution_convert_fusion
  270.8 5.6 %reshape.59 = bf16[8,496,248]{1,0,2:T(8,128)(2,1)S(1)} reshape(bf16[3968,248]{0,1:T(8,128)(2,1)} %convolution_convert_fusion) | data formatting | bytes 3936256 | tf_op jit(solution)/shard_map/reshape | solution.py:16
  276.4 0.7 copy.16
  277.0 28.4 %all_to_all.60 = bf16[8,496,248]{1,2,0:T(8,128)(2,1)S(1)} all-to-all(bf16[8,496,248]{1,2,0:T(8,128)(2,1)S(1)} %copy.16), channel_id=1, replica_groups=mesh['row'=16,'col'=8] {'col'}, dimensions={0} | all-to-all | bytes 3936256 | tf_op jit(solution)/shard_map/all_to_all | solution.py:22
  305.4 0.3 convert_reduce_fusion
  306.1 27.9 %all_to_all.61 = bf16[8,496,248]{2,1,0:T(8,128)(2,1)S(1)} all-to-all(bf16[8,496,248]{2,1,0:T(8,128)(2,1)S(1)} %broadcast_in_dim.31), channel_id=1, replica_groups=mesh['row'=16,'col'=8] {'col'}, dimensions={0} | all-to-all | bytes 3936256 | tf_op jit(solution)/shard_map/all_to_all | solution.py:34
  334.1 11.0 %convolution_convert_fusion.2 = bf16[416,2304]{1,0:T(8,128)(2,1)} fusion(s32[416]{0:T(512)S(1)} %subtract_add_fusion, pred[416]{0:T(512)(128)(4,1)S(1)} %fusion.16, bf16[3968,248]{1,0:T(8,128)(2,1)S(1)} %bitcast.31, bf16[3968,2304]{1,0:T(8,128)(2,1)} %all-gather.2.cloned.1.call-done, bf16[248,2304]{1,0:T(8,128)(2,1)S(1)} %copy-done), kind=kOutput, calls=%fused_computation.2 | convolution fusion | flops 5013986816 | bytes 23314464 | tf_op jit(solution)/shard_map/dot_general | solution.py:95
  345.1 1.7 all_to_all.48
  346.8 27.4 %all_to_all.62 = bf16[8,52,2304]{2,1,0:T(8,128)(2,1)S(1)} all-to-all(bf16[8,52,2304]{2,1,0:T(8,128)(2,1)S(1)} %all_to_all.48), channel_id=1, replica_groups=mesh['row'=16,'col'=8] {'col'}, dimensions={0} | all-to-all | bytes 3833856 | tf_op jit(solution)/shard_map/all_to_all | solution.py:98
  374.2 0.3 copy.18
  374.6 1.7 copy.20
  (19 shorter events, 1.3 us)
Async XLA Ops:
  10.2 5.7 %copy-start.1 = (s32[128]{0:T(128)S(1)}, s32[128]{0:T(128)}, u32[]{:S(2)}) copy-start(s32[128]{0:T(128)} %param.3) | copy-start | bytes 1540
  10.2 32.3 %all-to-all-start = ((bf16[52,8,2304]{2,0,1:T(8,128)(2,1)}), bf16[52,8,2304]{2,0,1:T(8,128)(2,1)S(1)}, u32[]{:S(2)}, u32[]{:S(2)}) async-start(bf16[52,8,2304]{2,0,1:T(8,128)(2,1)} %copy.14), calls=%async_computation | async-start | bytes 4128768 | tf_op jit(solution)/shard_map/all_to_all | solution.py:65
  15.9 147.6 %all-gather.2.cloned.1.call-start = ((), (), s32[]{:S(2)}) async-start(), calls=%async_computation.6 | async-start | bytes 19427328 | tf_op jit(solution)/shard_map/all_gather | solution.py:67
  306.1 28.0 %copy-start = (bf16[248,2304]{1,0:T(8,128)(2,1)S(1)}, bf16[248,2304]{1,0:T(8,128)(2,1)}, u32[]{:S(2)}) copy-start(bf16[248,2304]{1,0:T(8,128)(2,1)} %convolution_convert_fusion.3) | copy-start | bytes 3428356
Sparse Core Ops, SparseCore 0:
  47.4 116.0 all-gather.1
